TPU v7x, 256 devices: a whole 4x4x8 slice. The times are simulated.
256 devices in a mesh: item: 32 (over x, z), day: 8 (over y, core).
Axes of the slice: x: 4, y: 4, z: 8, core: 2. Of those that a mesh axis runs over, the one named last changes fastest.
Arguments:
- user_factors: float32 [2048, 512], P(('item', 'day')), may hold values from 0.005 to 0.012
- item_factors: bfloat16 [16384, 512], P('item'), may hold values from 0 to 1
- day_factors: bfloat16 [368, 512], P('day'), may hold values from 0.099609375 to 1
- tile_counts: bfloat16 [32768, 128, 128], P(('item', 'day')), may hold values from 0 to 23
- tile_index: int32 [3, 32768], P(None, ('item', 'day')), may hold values from 0 to 45, as said below
- tile_live: int32 [256], P(('item', 'day')), may hold values from 32 to 128, as said below
Outputs:
- updated_users: float32 [2048, 512], P(('item', 'day'))
Inputs may be any that keep to these rules, and one draw needn't show every extreme that they name: `tile_index`: row 0 names a user block below 16, row 1 an item block below 4 and row 2 a day below 46, local to the device that holds the slot. Only the first tile_live[d] slots of list d are live; some list has all 128 live.
All inputs are finite; a program needn't handle non-finite values.
Results may differ from a plain program's by a relative error of at most 0.003.
Values may be sent and summed in bfloat16 or wider, within the bound.
A program may use at most 64 MiB of HBM per device.

v0:
```python
import jax
import jax.numpy as jnp
from jax import lax
from jax.sharding import PartitionSpec as P

TILE = 128
GROUP = 8


def group_turns(phi, user_blocks, item_blocks, day_rows, counts, index, low, high):

    def turn(step, phi):
        start = step * GROUP
        tile_vals = lax.dynamic_slice_in_dim(counts, start, GROUP, 0)
        picks = lax.dynamic_slice_in_dim(index, start, GROUP, 1)
        places = start + jnp.arange(GROUP, dtype=jnp.int32)
        active = (places >= low) & (places < high)
        users = user_blocks[picks[0]]
        items = item_blocks[picks[1]]
        scales = day_rows[picks[2]].astype(jnp.float32)[:, None, :]
        scaled = (users.astype(jnp.float32) * scales).astype(jnp.bfloat16)
        model = jnp.einsum("gur,gir->gui", scaled, items, preferred_element_type=jnp.float32)
        ratio = jnp.where(active[:, None, None], tile_vals.astype(jnp.float32) / model, 0.0).astype(
            jnp.bfloat16
        )
        weighted = (items.astype(jnp.float32) * scales).astype(jnp.bfloat16)
        terms = jnp.einsum("gui,gir->gur", ratio, weighted, preferred_element_type=jnp.float32)
        return phi.at[picks[0]].add(terms)

    first = jnp.maximum(low, 0) // GROUP
    last = jnp.maximum((high + GROUP - 1) // GROUP, first)
    return lax.fori_loop(first, last, turn, phi)


def per_device(user_factors, item_factors, day_factors, tile_counts, tile_index, tile_live):
    rank = user_factors.shape[1]
    gathered = lax.all_gather(
        user_factors.astype(jnp.bfloat16), ("item", "day"), axis=0, tiled=True
    )
    user_blocks = gathered.reshape(-1, TILE, rank)
    item_blocks = item_factors.reshape(-1, TILE, rank)
    phi = jnp.zeros(user_blocks.shape, jnp.float32)
    own_count = tile_live[0]
    phi = group_turns(
        phi, user_blocks, item_blocks, day_factors, tile_counts, tile_index, 0, own_count
    )
    owned = lax.psum_scatter(
        phi.reshape(-1, rank), ("item", "day"), scatter_dimension=0, tiled=True
    )
    item_total = lax.psum(jnp.sum(item_factors.astype(jnp.float32), axis=0), "item")
    day_total = lax.psum(jnp.sum(day_factors.astype(jnp.float32), axis=0), "day")
    return user_factors * owned / (item_total * day_total)


def solution(mesh):
    in_specs = (
        P(("item", "day"), None),
        P("item", None),
        P("day", None),
        P(("item", "day"), None, None),
        P(None, ("item", "day")),
        P(("item", "day")),
    )
    out_specs = P(("item", "day"), None)
    return jax.shard_map(
        per_device, mesh=mesh, in_specs=in_specs, out_specs=out_specs, check_vma=False
    )
```

profile of v0, /device:TPU:0, one launch (start us, length us, event | category | flops | bytes accessed | tf_op | source)
XLA Modules:
  0.0 1605.5 jit_solution(8117053464810953249)
XLA Ops:
  8.6 107.7 %all-gather.2.cloned.1.call-done = bf16[2048,512]{1,0:T(8,128)(2,1)} async-done(((bf16[8,512]{1,0:T(8,128)(2,1)}), bf16[2048,512]{1,0:T(8,128)(2,1)}) %all-gather.2.cloned.1.call-update) | async-done | bytes 2097168 | tf_op jit(solution)/shard_map/all_gather | solution.py:37
  118.7 104.4 %while.10 = (s32[]{:T(128)}, f32[16,128,512]{2,1,0:T(8,128)}, s32[]{:T(128)}, s32[3,128]{1,0:T(4,128)S(1)}, s32[]{:T(128)}, /*index=5*/bf16[128,128,128]{2,1,0:T...) while((s32[]{:T(128)}, f32[16,128,512]{2,1,0:T(8,128)}, ...), condition=%wide.region_2.3_spmd, body=%wide.region_0.2_spmd.sunk | while | flops 272637024 | bytes 16078115 | solution.py:32
  121.1 3.2 gather_fusion.1
  127.6 4.1 scatter_fusion
  134.0 3.2 gather_fusion.1
  140.6 4.3 scatter_fusion
  147.1 3.2 gather_fusion.1
  153.7 4.2 scatter_fusion
  160.2 3.2 gather_fusion.1
  166.7 4.2 scatter_fusion
  173.2 3.2 gather_fusion.1
  177.0 2.7 fusion.20
  179.7 4.3 scatter_fusion
  186.3 3.2 gather_fusion.1
  192.8 4.2 scatter_fusion
  199.3 3.2 gather_fusion.1
  203.1 2.7 fusion.20
  205.8 4.2 scatter_fusion
  212.3 3.2 gather_fusion.1
  216.2 2.7 fusion.20
  218.9 4.2 scatter_fusion
  223.2 74.5 %psum.14 = f32[512]{0:T(512)S(1)} all-reduce(f32[512]{0:T(512)S(1)} %convert_reduce_fusion), channel_id=1, replica_groups=mesh['item'=32,'day'=8] {'item'}, use_global_device_ids=true, to_apply=%region_5.6 | all-reduce | flops 512 | bytes 4096 | tf_op jit(solution)/shard_map/psum | solution.py:50
  297.8 95.0 %psum.15 = f32[512]{0:T(512)S(1)} all-reduce(f32[512]{0:T(512)S(1)} %convert_reduce_fusion.1), channel_id=1, replica_groups=mesh['item'=32,'day'=8] {'day'}, use_global_device_ids=true, to_apply=%region_7.8 | all-reduce | flops 512 | bytes 4096 | tf_op jit(solution)/shard_map/psum | solution.py:51
  392.8 1204.5 %reduce-scatter.2.cloned.1.call-done = f32[8,512]{1,0:T(8,128)} async-done(((f32[2048,512]{1,0:T(8,128)}), f32[8,512]{1,0:T(8,128)}) %reduce-scatter.2.cloned.1.call-update) | async-done | bytes 16400 | tf_op jit(solution)/shard_map/reduce_scatter | solution.py:47
  (87 shorter events, 42.3 us)
Async XLA Ops:
  6.5 109.7 %all-gather.2.cloned.1.call-start = ((), (), s32[]{:S(2)}) async-start(), calls=%async_computation.1 | async-start | bytes 2105344 | tf_op jit(solution)/shard_map/all_gather | solution.py:37
  7.9 1589.4 %reduce-scatter.2.cloned.1.call-start = ((), (), s32[]{:S(2)}) async-start(), calls=%async_computation.2 | async-start | bytes 4210688 | tf_op jit(solution)/shard_map/reduce_scatter | solution.py:47
  116.3 2.5 copy-start
  116.3 2.5 copy-start.1
  116.3 2.5 copy-start.3
  223.1 1374.2 %copy-start.2 = (f32[8,512]{1,0:T(8,128)S(1)}, f32[8,512]{1,0:T(8,128)}, u32[]{:S(2)}) copy-start(f32[8,512]{1,0:T(8,128)} %param.8) | copy-start | bytes 49156
Sparse Core Ops, SparseCore 0:
  11.1 105.1 all-gather.1
  223.2 1374.0 reduce-scatter.1
where the time goes:
time: 1610 us
  waiting for transfers between devices  1310 us (81%)
  blocking collectives  170 us (11%)
  local copies, waits for them, and re-layouts  46 us (3%)
  other arithmetic  41.9 us (3%)
  matrix products  21.5 us (1%)
    reduce_scatter x1, waiting for transfers between devices, per_device(): lax.psum_scatter(phi.reshape(-1, rank), ('item', 'day'), scatter_dimensio...  1200 us
    all_gather x1, waiting for transfers between devices, per_device(): lax.all_gather(user_factors.astype(jnp.bfloat16), ('item', 'day'), axis=0...  108 us
    psum x1, blocking collectives, per_device(): lax.psum(jnp.sum(day_factors.astype(jnp.float32), axis=0), 'day')  95 us
    psum x1, blocking collectives, per_device(): lax.psum(jnp.sum(item_factors.astype(jnp.float32), axis=0), 'item')  74.5 us
    scatter-add x8, other arithmetic, turn(): return phi.at[picks[0]].add(terms)  33.7 us
  transfers between devices with their start and end apart: 2, of which 2 were waited for; matrix products, arithmetic and copies ran while one was open for 0% of the time, Pallas kernels for 0%

commit v1 on v0

--- a/solution.py
+++ b/solution.py
@@ -2,9 +2,17 @@
 import jax.numpy as jnp
 from jax import lax
 from jax.sharding import PartitionSpec as P
+from jax.lax import all_to_all, axis_size
 
 TILE = 128
 GROUP = 8
+
+
+def register_the_axis_part(u, mesh_name, d0):
+    clean = jnp.stack([u for _ in range(axis_size(mesh_name))])
+    plain = all_to_all(clean, mesh_name, 0, 0)
+    z_new = jnp.concatenate(plain, axis=d0)
+    return z_new
 
 
 def group_turns(phi, user_blocks, item_blocks, day_rows, counts, index, low, high):
@@ -34,9 +42,7 @@
 
 def per_device(user_factors, item_factors, day_factors, tile_counts, tile_index, tile_live):
     rank = user_factors.shape[1]
-    gathered = lax.all_gather(
-        user_factors.astype(jnp.bfloat16), ("item", "day"), axis=0, tiled=True
-    )
+    gathered = register_the_axis_part(user_factors.astype(jnp.bfloat16), ("item", "day"), 0)
     user_blocks = gathered.reshape(-1, TILE, rank)
     item_blocks = item_factors.reshape(-1, TILE, rank)
     phi = jnp.zeros(user_blocks.shape, jnp.float32)

time: 1610 us -> 1560 us (0.969)
  waiting for transfers between devices: 1310 us -> 1260 us
    all_gather x1 -> x0, waiting for transfers between devices: 108 us -> none  [per_device(): lax.all_gather(user_factors.astype(jnp.bfloat16), ('item', 'day'), axis=0...]
    all_to_all x0 -> x1, waiting for transfers between devices: none -> 50.3 us  [register_the_axis_part(): plain = all_to_all(clean, mesh_name, 0, 0)]
where the time goes in v1:
time: 1560 us
  waiting for transfers between devices  1260 us (81%)
  blocking collectives  167 us (11%)
  local copies, waits for them, and re-layouts  47.5 us (3%)
  other arithmetic  41.3 us (3%)
  matrix products  21.5 us (1%)
  starting transfers between devices  15.7 us (1%)
    reduce_scatter x1, waiting for transfers between devices, per_device(): lax.psum_scatter(phi.reshape(-1, rank), ('item', 'day'), scatter_dimensio...  1200 us
    psum x1, blocking collectives, per_device(): lax.psum(jnp.sum(day_factors.astype(jnp.float32), axis=0), 'day')  96.5 us
    psum x1, blocking collectives, per_device(): lax.psum(jnp.sum(item_factors.astype(jnp.float32), axis=0), 'item')  70.2 us
    all_to_all x1, waiting for transfers between devices, register_the_axis_part(): plain = all_to_all(clean, mesh_name, 0, 0)  50.3 us
    scatter-add x8, other arithmetic, turn(): return phi.at[picks[0]].add(terms)  33.7 us
  transfers between devices with their start and end apart: 2, of which 2 were waited for; matrix products, arithmetic and copies ran while one was open for 0% of the time, Pallas kernels for 0%

profile of v1, /device:TPU:0, one launch (start us, length us, event | category | flops | bytes accessed | tf_op | source)
XLA Modules:
  0.0 1562.2 jit_solution(9244035109112738977)
XLA Ops:
  8.7 15.6 %all-to-all-start = ((bf16[256,8,512]{2,1,0:T(8,128)(2,1)}), bf16[256,8,512]{2,1,0:T(8,128)(2,1)}, u32[]{:S(2)}, u32[]{:S(2)}) async-start(bf16[256,8,512]{2,1,0:T(8,128)(2,1)} %stack.2), calls=%async_computation | async-start | bytes 4194304 | tf_op jit(solution)/shard_map/all_to_all | solution.py:13
  25.1 50.3 %all-to-all-done = bf16[256,8,512]{2,1,0:T(8,128)(2,1)} async-done(((bf16[256,8,512]{2,1,0:T(8,128)(2,1)}), bf16[256,8,512]{2,1,0:T(8,128)(2,1)}, u32[]{:S(2)}, u32[]{:S(2)}) %all-to-all-start) | async-done | bytes 2097184 | tf_op jit(solution)/shard_map/all_to_all | solution.py:13
  77.9 104.4 %while.10 = (s32[]{:T(128)}, f32[16,128,512]{2,1,0:T(8,128)}, s32[]{:T(128)}, s32[3,128]{1,0:T(4,128)S(1)}, s32[]{:T(128)}, /*index=5*/bf16[128,128,128]{2,1,0:T...) while((s32[]{:T(128)}, f32[16,128,512]{2,1,0:T(8,128)}, ...), condition=%wide.region_2.3_spmd, body=%wide.region_0.2_spmd.sunk | while | flops 272637024 | bytes 16078115 | solution.py:40
  80.2 3.2 gather_fusion.1
  86.8 4.1 scatter_fusion
  93.2 3.2 gather_fusion.1
  99.7 4.3 scatter_fusion
  106.3 3.2 gather_fusion.1
  112.8 4.2 scatter_fusion
  119.4 3.2 gather_fusion.1
  123.2 2.7 fusion.20
  125.9 4.2 scatter_fusion
  132.4 3.2 gather_fusion.1
  136.2 2.7 fusion.20
  138.9 4.3 scatter_fusion
  145.5 3.2 gather_fusion.1
  152.0 4.2 scatter_fusion
  158.5 3.2 gather_fusion.1
  165.0 4.2 scatter_fusion
  171.5 3.2 gather_fusion.1
  178.1 4.2 scatter_fusion
  182.4 70.2 %psum.14 = f32[512]{0:T(512)S(1)} all-reduce(f32[512]{0:T(512)S(1)} %convert_reduce_fusion), channel_id=1, replica_groups=mesh['item'=32,'day'=8] {'item'}, use_global_device_ids=true, to_apply=%region_5.6 | all-reduce | flops 512 | bytes 4096 | tf_op jit(solution)/shard_map/psum | solution.py:56
  252.7 96.5 %psum.15 = f32[512]{0:T(512)S(1)} all-reduce(f32[512]{0:T(512)S(1)} %convert_reduce_fusion.1), channel_id=1, replica_groups=mesh['item'=32,'day'=8] {'day'}, use_global_device_ids=true, to_apply=%region_7.8 | all-reduce | flops 512 | bytes 4096 | tf_op jit(solution)/shard_map/psum | solution.py:57
  349.2 1204.8 %reduce-scatter.2.cloned.1.call-done = f32[8,512]{1,0:T(8,128)} async-done(((f32[2048,512]{1,0:T(8,128)}), f32[8,512]{1,0:T(8,128)}) %reduce-scatter.2.cloned.1.call-update) | async-done | bytes 16400 | tf_op jit(solution)/shard_map/reduce_scatter | solution.py:53
  (87 shorter events, 45.8 us)
Async XLA Ops:
  8.7 66.7 %all-to-all-start = ((bf16[256,8,512]{2,1,0:T(8,128)(2,1)}), bf16[256,8,512]{2,1,0:T(8,128)(2,1)}, u32[]{:S(2)}, u32[]{:S(2)}) async-start(bf16[256,8,512]{2,1,0:T(8,128)(2,1)} %stack.2), calls=%async_computation | async-start | bytes 4194304 | tf_op jit(solution)/shard_map/all_to_all | solution.py:13
  24.4 1529.7 %reduce-scatter.2.cloned.1.call-start = ((), (), s32[]{:S(2)}) async-start(), calls=%async_computation.2 | async-start | bytes 4210688 | tf_op jit(solution)/shard_map/reduce_scatter | solution.py:53
  75.4 2.5 copy-start
  75.4 2.5 copy-start.1
  75.4 2.5 copy-start.3
  182.3 1371.8 %copy-start.2 = (f32[8,512]{1,0:T(8,128)S(1)}, f32[8,512]{1,0:T(8,128)}, u32[]{:S(2)}) copy-start(f32[8,512]{1,0:T(8,128)} %param.8) | copy-start | bytes 49156
Sparse Core Ops, SparseCore 0:
  182.4 1371.5 reduce-scatter.1
